TPU v7x, 256 devices: a whole 4x4x8 slice. The times are simulated.
256 devices in a mesh: exp: 64 (over z, x, core), seq: 4 (over y).
Axes of the slice: x: 4, y: 4, z: 8, core: 2. Of those that a mesh axis runs over, the one named last changes fastest.
Arguments:
- layer_output_gradient: bfloat16 [2048, 7168], P(('exp', 'seq')), may hold values from -24 to 24
- residual_input: bfloat16 [2048, 7168], P(('exp', 'seq')), may hold values from -6 to 6
- norm_scale_vector: bfloat16 [7168], replicated, may hold values from 0.5 to 1.5
- chosen_expert_index: int32 [2048, 8], P(('exp', 'seq')), may hold values from 0 to 63, all different within a row; in each aligned block of 32 rows (0 to 31, 32 to 63, ...) at most 8 rows name the same one
- routing_gate_weight: bfloat16 [2048, 8], P(('exp', 'seq')), may hold values from 0.099609375 to 0.59765625
- expert_gate_weight: bfloat16 [64, 7168, 1024], P('exp', None, 'seq'), may hold values from -0.0625 to 0.0625
- expert_up_weight: bfloat16 [64, 7168, 1024], P('exp', None, 'seq'), may hold values from -0.0625 to 0.0625
- expert_down_weight: bfloat16 [64, 1024, 7168], P('exp', 'seq'), may hold values from -0.1875 to 0.1875
- stored_gate_state: bfloat16 [64, 512, 1024], P('exp', None, 'seq'), may hold values from -6 to 6
- stored_up_state: bfloat16 [64, 512, 1024], P('exp', None, 'seq'), may hold values from -6 to 6
- attention_output: bfloat16 [2048, 16384], P(('exp', 'seq')), may hold values from -24 to 24
- saved_adapter_latent: bfloat16 [2048, 32], P(('exp', 'seq')), may hold values from -0.109375 to 0.109375
- adapter_up_matrix: bfloat16 [32, 7168], replicated, may hold values from -0.00048828125 to 0.00048828125
Outputs:
- hidden_state_gradient: bfloat16 [2048, 7168], P(('exp', 'seq'))
- adapter_down_gradient: float32 [16384, 32], P(('exp', 'seq'))
- adapter_up_gradient_transposed: float32 [7168, 32], P(('exp', 'seq'))
Inputs may be any that keep to these rules, and one draw needn't show every extreme that they name: `chosen_expert_index`: each row names 8 different experts. In each aligned block of 32 rows (the tokens of one index of exp) no expert is named by more than 8 rows, and in some block some expert is named by exactly 8 rows.
All inputs are finite; a program needn't handle non-finite values.
Results may differ from a plain program's by a relative error of at most 0.015.
Values may be sent and summed in bfloat16 or wider, within the bound.
A program may use at most 128 MiB of HBM per device.

v0:
```python
import jax
import jax.numpy as jnp
from jax import lax
from jax.sharding import PartitionSpec as P

ADAPTER_SCALE = 2.0
NORM_EPS = 1e-06


def silu_parts(gate_val):
    sigmoid_val = jax.nn.sigmoid(gate_val)
    return (gate_val * sigmoid_val, sigmoid_val * (1.0 + gate_val * (1.0 - sigmoid_val)))


def contract_trailing(left, right):
    return lax.dot_general(
        left, right, (((1,), (1,)), ((), ())), preferred_element_type=jnp.float32
    )


def contract_leading(left, right):
    return lax.dot_general(
        left, right, (((0,), (0,)), ((), ())), preferred_element_type=jnp.float32
    )


def per_device(
    layer_output_gradient,
    residual_input,
    norm_scale_vector,
    chosen_expert_index,
    routing_gate_weight,
    expert_gate_weight,
    expert_up_weight,
    expert_down_weight,
    stored_gate_state,
    stored_up_state,
    attention_output,
    saved_adapter_latent,
    adapter_up_matrix,
):
    model_width = layer_output_gradient.shape[1]
    experts = lax.axis_size("exp") * expert_gate_weight.shape[0]
    capacity = stored_gate_state.shape[1] // experts
    group_grad, group_ids, group_weights = (
        lax.all_gather(layer_output_gradient, "seq", axis=0, tiled=True),
        lax.all_gather(chosen_expert_index, "seq", axis=0, tiled=True),
        lax.all_gather(routing_gate_weight, "seq", axis=0, tiled=True),
    )
    group_size = group_grad.shape[0]
    top_count = group_ids.shape[1]
    labels = jnp.arange(experts, dtype=jnp.int32)
    named_by = jnp.sum((group_ids[:, :, None] == labels[None, None, :]).astype(jnp.int32), axis=1)
    before = jnp.cumsum(named_by, axis=0) - named_by
    position = jnp.take_along_axis(before, group_ids, axis=1)
    slot_index = (group_ids * capacity + position).reshape(-1).astype(jnp.int32)
    token_ids = jnp.repeat(jnp.arange(group_size, dtype=jnp.int32), top_count)
    slot_owner = (
        jnp.full((experts * capacity,), group_size, jnp.int32).at[slot_index].set(token_ids)
    )
    padded = jnp.concatenate([group_grad, jnp.zeros((1, model_width), group_grad.dtype)], axis=0)
    outgoing = padded[slot_owner].reshape(experts, capacity, model_width)
    incoming = lax.all_to_all(outgoing, "exp", split_axis=0, concat_axis=0, tiled=True)
    slot_rows = incoming.reshape(-1, model_width)
    hidden_grad = contract_trailing(slot_rows, expert_down_weight[0])
    activation, silu_slope = silu_parts(stored_gate_state[0].astype(jnp.float32))
    gate_grad = (hidden_grad * stored_up_state[0].astype(jnp.float32) * silu_slope).astype(
        jnp.bfloat16
    )
    up_grad = (hidden_grad * activation).astype(jnp.bfloat16)
    partial_value = (
        contract_trailing(gate_grad, expert_gate_weight[0])
        + contract_trailing(up_grad, expert_up_weight[0])
    ).astype(jnp.bfloat16)
    sources = partial_value.shape[0] // capacity
    weights = group_weights.astype(jnp.float32)
    returned = lax.all_to_all(
        partial_value.reshape(sources, capacity, model_width),
        "exp",
        split_axis=0,
        concat_axis=0,
        tiled=True,
    )
    combine_returned = returned.reshape(experts * capacity, model_width)
    picked = combine_returned[slot_index].reshape(group_size, top_count, -1).astype(jnp.float32)
    combined = jnp.sum(picked * weights[:, :, None], axis=1)
    moe_grad = lax.psum_scatter(
        combined.astype(jnp.bfloat16), "seq", scatter_dimension=0, tiled=True
    ).astype(jnp.float32)
    residual = residual_input.astype(jnp.float32)
    inverse_rms = lax.rsqrt(jnp.mean(residual * residual, axis=1, keepdims=True) + NORM_EPS)
    scaled = norm_scale_vector.astype(jnp.float32)[None, :] * moe_grad
    inner_mean = jnp.mean(scaled * residual, axis=1, keepdims=True)
    hidden_state_gradient = (
        layer_output_gradient.astype(jnp.float32)
        + inverse_rms * scaled
        - residual * inner_mean * inverse_rms**3
    ).astype(jnp.bfloat16)
    adapter_latent_value = (
        ADAPTER_SCALE * contract_trailing(hidden_state_gradient, adapter_up_matrix)
    ).astype(jnp.bfloat16)
    down_contribution = contract_leading(attention_output, adapter_latent_value)
    up_contribution = ADAPTER_SCALE * contract_leading(hidden_state_gradient, saved_adapter_latent)
    complete_down_matrix, complete_up_matrix = lax.psum(
        (down_contribution, up_contribution), ("exp", "seq")
    )
    slot_member = lax.axis_index(("exp", "seq"))
    members = lax.axis_size(("exp", "seq"))
    down_projection_rows = complete_down_matrix.shape[0] // members
    up_projection_rows = complete_up_matrix.shape[0] // members
    adapter_down_gradient = lax.dynamic_slice_in_dim(
        complete_down_matrix, slot_member * down_projection_rows, down_projection_rows, 0
    )
    adapter_up_gradient_transposed = lax.dynamic_slice_in_dim(
        complete_up_matrix, slot_member * up_projection_rows, up_projection_rows, 0
    )
    return (hidden_state_gradient, adapter_down_gradient, adapter_up_gradient_transposed)


def solution(mesh):
    return jax.shard_map(
        per_device,
        mesh=mesh,
        in_specs=(
            P(("exp", "seq"), None),
            P(("exp", "seq"), None),
            P(),
            P(("exp", "seq"), None),
            P(("exp", "seq"), None),
            P("exp", None, "seq"),
            P("exp", None, "seq"),
            P("exp", "seq", None),
            P("exp", None, "seq"),
            P("exp", None, "seq"),
            P(("exp", "seq"), None),
            P(("exp", "seq"), None),
            P(),
        ),
        out_specs=(P(("exp", "seq"), None), P(("exp", "seq"), None), P(("exp", "seq"), None)),
        check_vma=False,
    )
```

profile of v0, /device:TPU:2, one launch (start us, length us, event | category | flops | bytes accessed | tf_op | source)
XLA Modules:
  0.0 736.5 jit_solution(16224991714569872756)
XLA Ops:
  7.2 12.7 %all_gather.10 = s32[32,8]{1,0:T(8,128)S(1)} all-gather(s32[8,8]{1,0:T(8,128)} %param.16), channel_id=1, replica_groups=mesh['exp'=64,'seq'=4] {'seq'}, dimensions={0}, use_global_device_ids=true | all-gather | bytes 1280 | tf_op jit(solution)/shard_map/all_gather | solution.py:47
  19.9 0.1 convert_reduce_fusion
  20.2 1.9 gather_fusion.2
  22.3 0.1 reshape.90
  22.5 1.4 scatter_custom_fusion
  23.9 12.7 %all_gather.9 = bf16[32,7168]{1,0:T(8,128)(2,1)S(1)} all-gather(bf16[8,7168]{1,0:T(8,128)(2,1)S(1)} %copy-done.6), channel_id=1, replica_groups=mesh['exp'=64,'seq'=4] {'seq'}, dimensions={0}, use_global_device_ids=true | all-gather | bytes 573440 | tf_op jit(solution)/shard_map/all_gather | solution.py:46
  36.6 7.1 gather_fusion
  43.6 175.9 %all_to_all.10 = bf16[64,8,7168]{2,1,0:T(8,128)(2,1)S(1)} all-to-all(bf16[64,8,7168]{2,1,0:T(8,128)(2,1)} %bitcast.47), channel_id=1, replica_groups=mesh['exp'=64,'seq'=4] {'exp'}, dimensions={0} | all-to-all | bytes 14680064 | tf_op jit(solution)/shard_map/all_to_all | solution.py:63
  219.6 2.1 fusion.2
  221.7 7.4 %fusion.5 = f32[512,7168]{1,0:T(8,128)} fusion(bf16[1,7168,256]{2,1,0:T(8,128)(2,1)S(1)} %copy-done.1, f32[512,256]{1,0:T(8,128)S(1)} %fusion.2, bf16[1,512,256]{2,1,0:T(8,128)(2,1)S(1)} %copy-done.7, bf16[1,512,256]{2,1,0:T(8,128)(2,1)S(1)} %copy-done.3), kind=kOutput, calls=%fused_computation.13 | convolution fusion | flops 1880621056 | bytes 19398656 | tf_op jit(solution)/shard_map/dot_general | solution.py:16
  229.1 10.3 %fusion = bf16[64,8,7168]{2,1,0:T(8,128)(2,1)} fusion(f32[512,7168]{1,0:T(8,128)} %fusion.5, bf16[1,7168,256]{2,1,0:T(8,128)(2,1)S(1)} %copy-done.2, f32[512,256]{1,0:T(8,128)S(1)} %fusion.2, bf16[1,512,256]{2,1,0:T(8,128)(2,1)S(1)} %copy-done.3), kind=kOutput, calls=%fused_computation.6 | convolution fusion | flops 1887305728 | bytes 26476544 | tf_op jit(solution)/shard_map/dot_general | solution.py:16
  239.4 6.0 all-to-all-start.1
  245.4 10.6 %all_gather.11 = bf16[32,8]{1,0:T(8,128)(2,1)S(1)} all-gather(bf16[8,8]{1,0:T(8,128)(2,1)S(1)} %copy-done.11), channel_id=1, replica_groups=mesh['exp'=64,'seq'=4] {'seq'}, dimensions={0}, use_global_device_ids=true | all-gather | bytes 640 | tf_op jit(solution)/shard_map/all_gather | solution.py:48
  256.0 151.7 %all-to-all-done.1 = bf16[64,8,7168]{2,1,0:T(8,128)(2,1)} async-done(((bf16[64,8,7168]{2,1,0:T(8,128)(2,1)}), bf16[64,8,7168]{2,1,0:T(8,128)(2,1)}, u32[]{:S(2)}, u32[]{:S(2)}) %all-to-all-start.1) | async-done | bytes 7340064 | tf_op jit(solution)/shard_map/all_to_all | solution.py:77
  407.7 12.1 %gather_fusion.1 = bf16[256,7168]{1,0:T(8,128)(2,1)} fusion(bf16[512,7168]{1,0:T(8,128)(2,1)} %bitcast.11, s32[1024]{0:T(1024)S(1)} %pad_clamp_fusion), kind=kCustom, calls=%fused_computation.1 | custom fusion | bytes 7341056 | tf_op jit(solution)/shard_map/gather | solution.py:85
  419.9 5.5 fusion.1
  425.4 21.3 %reduce-scatter.2.cloned.1.call-done = bf16[8,7168]{1,0:T(8,128)(2,1)} async-done(((bf16[32,7168]{1,0:T(8,128)(2,1)}), bf16[8,7168]{1,0:T(8,128)(2,1)}) %reduce-scatter.2.cloned.1.call-update) | async-done | bytes 114704 | tf_op jit(solution)/shard_map/reduce_scatter | solution.py:87
  446.7 1.1 fusion.26
  447.8 1.0 fusion.29
  448.9 2.7 convolution_multiply_fusion
  451.6 2.3 convolution_bitcast_fusion
  453.9 273.0 %all-reduce.4.cloned.1.call-done = (f32[16384,32]{0,1:T(8,128)}, f32[7168,32]{1,0:T(8,128)}) async-done(((f32[16384,32]{0,1:T(8,128)}, f32[7168,32]{1,0:T(8,128)}), (f32[16384,32]{0,1:T(8,128)}, f32[7168,32]{1,0:T(8,128)})) %all-reduce.4.cloned.1.call-update) | async-done | bytes 3014672 | tf_op jit(solution)/shard_map/psum | solution.py:104
  726.9 1.3 constant_dynamic-slice_fusion
  728.3 1.4 constant_dynamic-slice_fusion.1
  (46 shorter events, 0.6 us)
Async XLA Ops:
  7.2 444.4 %copy-start = (bf16[32,7168]{1,0:T(8,128)(2,1)S(1)}, bf16[32,7168]{1,0:T(8,128)(2,1)}, u32[]{:S(2)}) copy-start(bf16[32,7168]{1,0:T(8,128)(2,1)} %param.25) | copy-start | bytes 1376260
  20.2 3.7 copy-start.6
  43.6 175.9 %copy-start.12 = (bf16[1,256,7168]{2,1,0:T(8,128)(2,1)S(1)}, bf16[1,256,7168]{2,1,0:T(8,128)(2,1)}, u32[]{:S(2)}) copy-start(bf16[1,256,7168]{2,1,0:T(8,128)(2,1)} %param.20) | copy-start | bytes 11010052
  219.5 2.1 copy-start.1
  219.6 2.1 copy-start.3
  219.6 2.1 copy-start.7
  221.7 7.4 %copy-start.2 = (bf16[1,7168,256]{2,1,0:T(8,128)(2,1)S(1)}, bf16[1,7168,256]{2,1,0:T(8,128)(2,1)}, u32[]{:S(2)}) copy-start(bf16[1,7168,256]{2,1,0:T(8,128)(2,1)} %param.19) | copy-start | bytes 11010052
  239.4 6.0 copy-start.11
  239.4 168.3 %all-to-all-start.1 = ((bf16[64,8,7168]{2,1,0:T(8,128)(2,1)}), bf16[64,8,7168]{2,1,0:T(8,128)(2,1)}, u32[]{:S(2)}, u32[]{:S(2)}) async-start(bf16[64,8,7168]{2,1,0:T(8,128)(2,1)} %fusion), calls=%async_computation.1 | async-start | bytes 14680064 | tf_op jit(solution)/shard_map/all_to_all | solution.py:77
  245.4 201.3 %reduce-scatter.2.cloned.1.call-start = ((), (), s32[]{:S(2)}) async-start(), calls=%async_computation.3 | async-start | bytes 573440 | tf_op jit(solution)/shard_map/reduce_scatter | solution.py:87
  419.9 5.6 copy-start.9
  419.9 26.9 %copy-start.5 = (bf16[8,7168]{1,0:T(8,128)(2,1)S(1)}, bf16[8,7168]{1,0:T(8,128)(2,1)}, u32[]{:S(2)}) copy-start(bf16[8,7168]{1,0:T(8,128)(2,1)} %param.14) | copy-start | bytes 344068
  419.9 29.0 %copy-start.10 = (bf16[8,32]{1,0:T(8,128)(2,1)S(1)}, bf16[8,32]{1,0:T(8,128)(2,1)}, u32[]{:S(2)}) copy-start(bf16[8,32]{1,0:T(8,128)(2,1)} %param.24) | copy-start | bytes 1540
  419.9 31.7 %copy-start.8 = (bf16[8,16384]{1,0:T(8,128)(2,1)S(1)}, bf16[8,16384]{1,0:T(8,128)(2,1)}, u32[]{:S(2)}) copy-start(bf16[8,16384]{1,0:T(8,128)(2,1)} %param.23) | copy-start | bytes 786436
  425.4 301.6 %all-reduce.4.cloned.1.call-start = ((), (), s32[]{:S(2)}) async-start(), calls=%async_computation.4 | async-start | bytes 11534336 | tf_op jit(solution)/shard_map/psum | solution.py:104
  448.9 5.0 copy-start.4
Sparse Core Ops, SparseCore 0:
  425.5 21.1 reduce-scatter.1
  454.0 272.8 all-reduce.3
where the time goes:
time: 737 us; the launch traced here: 736 us
  waiting for transfers between devices  446 us (61%)
  blocking collectives  212 us (29%)
  local copies, waits for them, and re-layouts  25.7 us (3%)
  matrix products  24.7 us (3%)
  between operations  14.3 us (2%)
  other arithmetic  7.84 us (1%)
    psum x1, waiting for transfers between devices, per_device(): lax.psum((down_contribution, up_contribution), ('exp', 'seq'))  273 us
    all_to_all x1, blocking collectives, per_device(): lax.all_to_all(outgoing, 'exp', split_axis=0, concat_axis=0, tiled=True)  176 us
    all_to_all x1, waiting for transfers between devices, per_device(): lax.all_to_all(partial_value.reshape(sources, capacity, model_width), 'ex...  152 us
    reduce_scatter x1, waiting for transfers between devices, per_device(): lax.psum_scatter(combined.astype(jnp.bfloat16), 'seq', scatter_dimension=...  21.3 us
    dot_general x3, matrix products, contract_trailing(): lax.dot_general(left, right, (((1,), (1,)), ((), ())), preferred_element_...  19.8 us
  transfers between devices with their start and end apart: 3, of which 3 were waited for; matrix products, arithmetic and copies ran while one was open for 0% of the time, Pallas kernels for 0%

commit v1 on v0

--- a/solution.py
+++ b/solution.py
@@ -102,7 +102,7 @@
     down_contribution = contract_leading(attention_output, adapter_latent_value)
     up_contribution = ADAPTER_SCALE * contract_leading(hidden_state_gradient, saved_adapter_latent)
     complete_down_matrix, complete_up_matrix = lax.psum(
-        (down_contribution, up_contribution), ("exp", "seq")
+        lax.psum((down_contribution, up_contribution), "seq"), "exp"
     )
     slot_member = lax.axis_index(("exp", "seq"))
     members = lax.axis_size(("exp", "seq"))

time: 737 us -> 791 us (1.073)
  waiting for transfers between devices: 446 us -> 500 us
    psum x1 -> x2, waiting for transfers between devices: 273 us -> 327 us  [the longest x1 203 us: per_device(): lax.psum(lax.psum((down_contribution, up_contribution), 'seq'), 'exp')]
  transfers between devices with their start and end apart: 3 -> 4, of which waited for: 3 -> 4; matrix products, arithmetic and copies ran while one was open for 0% -> 0% of each run, Pallas kernels for 0% -> 0%
where the time goes in v1:
time: 791 us; the launch traced here: 790 us
  waiting for transfers between devices  500 us (63%)
  blocking collectives  212 us (27%)
  local copies, waits for them, and re-layouts  25.7 us (3%)
  matrix products  24.7 us (3%)
  between operations  14 us (2%)
    psum x1, waiting for transfers between devices, per_device(): lax.psum(lax.psum((down_contribution, up_contribution), 'seq'), 'exp')  203 us
    all_to_all x1, blocking collectives, per_device(): lax.all_to_all(outgoing, 'exp', split_axis=0, concat_axis=0, tiled=True)  176 us
    all_to_all x1, waiting for transfers between devices, per_device(): lax.all_to_all(partial_value.reshape(sources, capacity, model_width), 'ex...  152 us
    psum x1, waiting for transfers between devices, per_device(): lax.psum((down_contribution, up_contribution), 'seq')  124 us
    reduce_scatter x1, waiting for transfers between devices, per_device(): lax.psum_scatter(combined.astype(jnp.bfloat16), 'seq', scatter_dimension=...  21.3 us
    dot_general x3, matrix products, contract_trailing(): lax.dot_general(left, right, (((1,), (1,)), ((), ())), preferred_element_...  19.8 us
  transfers between devices with their start and end apart: 4, of which 4 were waited for; matrix products, arithmetic and copies ran while one was open for 0% of the time, Pallas kernels for 0%

profile of v1, /device:TPU:2, one launch (start us, length us, event | category | flops | bytes accessed | tf_op | source)
XLA Modules:
  0.0 789.9 jit_solution(16030901956927473295)
XLA Ops:
  7.2 12.7 %all_gather.10 = s32[32,8]{1,0:T(8,128)S(1)} all-gather(s32[8,8]{1,0:T(8,128)} %param.16), channel_id=1, replica_groups=mesh['exp'=64,'seq'=4] {'seq'}, dimensions={0}, use_global_device_ids=true | all-gather | bytes 1280 | tf_op jit(solution)/shard_map/all_gather | solution.py:47
  19.9 0.1 convert_reduce_fusion
  20.2 1.9 gather_fusion.2
  22.5 1.4 scatter_custom_fusion
  23.9 12.7 %all_gather.9 = bf16[32,7168]{1,0:T(8,128)(2,1)S(1)} all-gather(bf16[8,7168]{1,0:T(8,128)(2,1)S(1)} %copy-done.6), channel_id=1, replica_groups=mesh['exp'=64,'seq'=4] {'seq'}, dimensions={0}, use_global_device_ids=true | all-gather | bytes 573440 | tf_op jit(solution)/shard_map/all_gather | solution.py:46
  36.6 7.1 gather_fusion
  43.7 175.9 %all_to_all.10 = bf16[64,8,7168]{2,1,0:T(8,128)(2,1)S(1)} all-to-all(bf16[64,8,7168]{2,1,0:T(8,128)(2,1)} %bitcast.47), channel_id=1, replica_groups=mesh['exp'=64,'seq'=4] {'exp'}, dimensions={0} | all-to-all | bytes 14680064 | tf_op jit(solution)/shard_map/all_to_all | solution.py:63
  219.6 2.1 fusion.2
  221.7 7.4 fusion.5
  229.2 10.3 %fusion = bf16[64,8,7168]{2,1,0:T(8,128)(2,1)} fusion(f32[512,7168]{1,0:T(8,128)} %fusion.5, bf16[1,7168,256]{2,1,0:T(8,128)(2,1)S(1)} %copy-done.2, f32[512,256]{1,0:T(8,128)S(1)} %fusion.2, bf16[1,512,256]{2,1,0:T(8,128)(2,1)S(1)} %copy-done.3), kind=kOutput, calls=%fused_computation.6 | convolution fusion | flops 1887305728 | bytes 26476544 | tf_op jit(solution)/shard_map/dot_general | solution.py:16
  239.4 6.0 all-to-all-start.1
  245.4 10.6 %all_gather.11 = bf16[32,8]{1,0:T(8,128)(2,1)S(1)} all-gather(bf16[8,8]{1,0:T(8,128)(2,1)S(1)} %copy-done.11), channel_id=1, replica_groups=mesh['exp'=64,'seq'=4] {'seq'}, dimensions={0}, use_global_device_ids=true | all-gather | bytes 640 | tf_op jit(solution)/shard_map/all_gather | solution.py:48
  256.0 151.7 %all-to-all-done.1 = bf16[64,8,7168]{2,1,0:T(8,128)(2,1)} async-done(((bf16[64,8,7168]{2,1,0:T(8,128)(2,1)}), bf16[64,8,7168]{2,1,0:T(8,128)(2,1)}, u32[]{:S(2)}, u32[]{:S(2)}) %all-to-all-start.1) | async-done | bytes 7340064 | tf_op jit(solution)/shard_map/all_to_all | solution.py:77
  407.7 12.1 %gather_fusion.1 = bf16[256,7168]{1,0:T(8,128)(2,1)} fusion(bf16[512,7168]{1,0:T(8,128)(2,1)} %bitcast.11, s32[1024]{0:T(1024)S(1)} %pad_clamp_fusion), kind=kCustom, calls=%fused_computation.1 | custom fusion | bytes 7341056 | tf_op jit(solution)/shard_map/gather | solution.py:85
  419.9 5.5 fusion.1
  425.4 21.3 %reduce-scatter.2.cloned.1.call-done = bf16[8,7168]{1,0:T(8,128)(2,1)} async-done(((bf16[32,7168]{1,0:T(8,128)(2,1)}), bf16[8,7168]{1,0:T(8,128)(2,1)}) %reduce-scatter.2.cloned.1.call-update) | async-done | bytes 114704 | tf_op jit(solution)/shard_map/reduce_scatter | solution.py:87
  446.7 1.1 fusion.26
  447.8 1.0 fusion.29
  448.9 2.7 convolution_multiply_fusion
  451.6 2.2 convolution_bitcast_fusion
  453.9 123.5 %all-reduce.8.cloned.1.call-done = (f32[16384,32]{0,1:T(8,128)}, f32[7168,32]{1,0:T(8,128)}) async-done(((f32[16384,32]{0,1:T(8,128)}, f32[7168,32]{1,0:T(8,128)}), (f32[16384,32]{0,1:T(8,128)}, f32[7168,32]{1,0:T(8,128)})) %all-reduce.8.cloned.1.call-update) | async-done | bytes 3014672 | tf_op jit(solution)/shard_map/psum | solution.py:105
  577.5 203.1 %all-reduce.6.cloned.1.call-done = (f32[16384,32]{0,1:T(8,128)}, f32[7168,32]{1,0:T(8,128)}) async-done(((f32[16384,32]{0,1:T(8,128)}, f32[7168,32]{1,0:T(8,128)}), (f32[16384,32]{0,1:T(8,128)}, f32[7168,32]{1,0:T(8,128)})) %all-reduce.6.cloned.1.call-update) | async-done | bytes 3014672 | tf_op jit(solution)/shard_map/psum | solution.py:104
  780.6 1.3 constant_dynamic-slice_fusion
  781.9 1.4 constant_dynamic-slice_fusion.1
  (49 shorter events, 0.7 us)
Async XLA Ops:
  7.2 444.4 %copy-start = (bf16[32,7168]{1,0:T(8,128)(2,1)S(1)}, bf16[32,7168]{1,0:T(8,128)(2,1)}, u32[]{:S(2)}) copy-start(bf16[32,7168]{1,0:T(8,128)(2,1)} %param.25) | copy-start | bytes 1376260
  20.2 3.7 copy-start.6
  43.7 175.9 %copy-start.12 = (bf16[1,256,7168]{2,1,0:T(8,128)(2,1)S(1)}, bf16[1,256,7168]{2,1,0:T(8,128)(2,1)}, u32[]{:S(2)}) copy-start(bf16[1,256,7168]{2,1,0:T(8,128)(2,1)} %param.20) | copy-start | bytes 11010052
  219.6 2.1 copy-start.1
  219.6 2.1 copy-start.3
  219.6 2.1 copy-start.7
  221.7 7.5 copy-start.2
  239.4 6.0 copy-start.11
  239.4 168.3 %all-to-all-start.1 = ((bf16[64,8,7168]{2,1,0:T(8,128)(2,1)}), bf16[64,8,7168]{2,1,0:T(8,128)(2,1)}, u32[]{:S(2)}, u32[]{:S(2)}) async-start(bf16[64,8,7168]{2,1,0:T(8,128)(2,1)} %fusion), calls=%async_computation.1 | async-start | bytes 14680064 | tf_op jit(solution)/shard_map/all_to_all | solution.py:77
  245.4 201.3 %reduce-scatter.2.cloned.1.call-start = ((), (), s32[]{:S(2)}) async-start(), calls=%async_computation.3 | async-start | bytes 573440 | tf_op jit(solution)/shard_map/reduce_scatter | solution.py:87
  419.9 5.5 copy-start.9
  419.9 26.9 %copy-start.5 = (bf16[8,7168]{1,0:T(8,128)(2,1)S(1)}, bf16[8,7168]{1,0:T(8,128)(2,1)}, u32[]{:S(2)}) copy-start(bf16[8,7168]{1,0:T(8,128)(2,1)} %param.14) | copy-start | bytes 344068
  419.9 29.0 %copy-start.10 = (bf16[8,32]{1,0:T(8,128)(2,1)S(1)}, bf16[8,32]{1,0:T(8,128)(2,1)}, u32[]{:S(2)}) copy-start(bf16[8,32]{1,0:T(8,128)(2,1)} %param.24) | copy-start | bytes 1540
  419.9 31.7 %copy-start.8 = (bf16[8,16384]{1,0:T(8,128)(2,1)S(1)}, bf16[8,16384]{1,0:T(8,128)(2,1)}, u32[]{:S(2)}) copy-start(bf16[8,16384]{1,0:T(8,128)(2,1)} %param.23) | copy-start | bytes 786436
  425.4 152.1 %all-reduce.8.cloned.1.call-start = ((), (), s32[]{:S(2)}) async-start(), calls=%async_computation.5 | async-start | bytes 11534336 | tf_op jit(solution)/shard_map/psum | solution.py:105
  448.9 5.0 copy-start.4
  453.9 326.7 %all-reduce.6.cloned.1.call-start = ((), (), s32[]{:S(2)}) async-start(), calls=%async_computation.4 | async-start | bytes 11534336 | tf_op jit(solution)/shard_map/psum | solution.py:104
Sparse Core Ops, SparseCore 0:
  425.5 21.1 reduce-scatter.1
  454.0 123.3 all-reduce.7
  581.6 198.9 all-reduce.5
